TPU v7x, 256 devices: a whole 4x4x8 slice. The times are simulated.
256 devices in a mesh: dp: 64 (over x, z, y_lo), seq: 4 (over y_hi, core).
Axes of the slice: x: 4, y: 4 (y_hi: 2, y_lo: 2; y = y_hi * 2 + y_lo), z: 8, core: 2. Of those that a mesh axis runs over, the one named last changes fastest.
Arguments:
- block_input: float32 [128, 512, 768], P('dp', 'seq'), may hold values from -6 to 6
- doc_ids: int32 [128, 512], P('dp'), may hold values from 0 to 2, as said below
- positions: int32 [128, 512], P('dp', 'seq'), may hold values from 0 to 509, as said below
- w_qkv: bfloat16 [768, 2304], P(('dp', 'seq')), may hold values from -0.21875 to 0.21875
- w_out: bfloat16 [768, 768], P(('dp', 'seq')), may hold values from -2.5 to 2.5
- w_in: bfloat16 [768, 2304], P(('dp', 'seq')), may hold values from -0.21875 to 0.21875
- w_down: bfloat16 [768, 1152], P(('dp', 'seq')), may hold values from -0.1875 to 0.1875
- gain_attn: bfloat16 [768], P(('dp', 'seq')), may hold values from 0.099609375 to 1.8984375
- gain_ffn: bfloat16 [768], P(('dp', 'seq')), may hold values from 0.099609375 to 1.8984375
- cotangent: float32 [128, 512, 768], P('dp', 'seq'), may hold values from -16 to 16
Outputs:
- block_output: float32 [128, 512, 768], P('dp', 'seq')
- input_grad: float32 [128, 512, 768], P('dp', 'seq')
- grad_qkv: float32 [768, 2304], P(('dp', 'seq'))
- grad_out: float32 [768, 768], P(('dp', 'seq'))
- grad_in: float32 [768, 2304], P(('dp', 'seq'))
- grad_down: float32 [768, 1152], P(('dp', 'seq'))
- grad_gain_attn: float32 [768], P(('dp', 'seq'))
- grad_gain_ffn: float32 [768], P(('dp', 'seq'))
Inputs may be any that keep to these rules, and one draw needn't show every extreme that they name: `doc_ids`: every sequence holds exactly 3 documents, each a run of tokens, with ids 0 to 2 in order; the boundaries differ from sequence to sequence. `positions`: a token's position counted from the first token of its document.
All inputs are finite; a program needn't handle non-finite values.
Results may differ from a plain program's by a relative error of at most 0.02.
Values may be sent and summed in bfloat16 or wider, within the bound.
A program may use at most 128 MiB of HBM per device.

v0:
```python
import math
import jax
import jax.numpy as jnp
from jax import lax
from jax.sharding import PartitionSpec as P

D = 768
H = 12
HD = 64
FF = 1152
norm_eps = 1e-05
rope_base = 160000.0


def in_one_piece(arrays, axis, dim, along):
    widths = [math.prod(a.shape[along:]) for a in arrays]
    both = jnp.concatenate(
        [a.reshape(*a.shape[:along], w) for a, w in zip(arrays, widths)], axis=along
    )
    filled = lax.all_gather(both, axis, axis=dim, tiled=True)
    blocks = jnp.split(filled, [sum(widths[:k]) for k in range(1, len(widths))], axis=along)
    return tuple(
        (b.reshape(*filled.shape[:along], *a.shape[along:]) for a, b in zip(arrays, blocks))
    )


def sent_together(arrays, axis, dim, along):
    ends, at = ([], 0)
    for a in arrays[:-1]:
        at += a.shape[along]
        ends.append(at)
    both = jnp.concatenate(arrays, axis=along)
    return tuple(
        jnp.split(lax.psum_scatter(both, axis, scatter_dimension=dim, tiled=True), ends, axis=along)
    )


def side_by_side(arrays, axis, dim, along):
    both = jnp.concatenate(arrays, axis=along)
    filled, at, done = (lax.all_gather(both, axis, axis=dim, tiled=True), 0, [])
    for a in arrays:
        done.append(lax.slice_in_dim(filled, at, at + a.shape[along], axis=along))
        at += a.shape[along]
    return tuple(done)


def cut_along(shard, dim, peers):
    shape = shard.shape
    blocks = shard.reshape(*shape[:dim], peers, shape[dim] // peers, *shape[dim + 1 :])
    return jnp.moveaxis(blocks, dim, 0)


def sent_and_summed(shard, axis, dim):
    peers = lax.axis_size(axis)
    blocks = lax.all_to_all(cut_along(shard, dim, peers), axis, 0, 0, tiled=True)
    return jnp.sum(blocks, axis=0)


def in_one_piece_2(arrays, axis, dim, along):
    widths = [a.shape[along] for a in arrays]
    both = jnp.concatenate(arrays, axis=along)
    filled = sent_and_summed(both, axis, dim)
    return tuple(jnp.split(filled, [sum(widths[:k]) for k in range(1, len(widths))], axis=along))


def normalize(matrix):
    center = matrix - jnp.mean(matrix, axis=-1, keepdims=True)
    inverse = lax.rsqrt(jnp.mean(center * center, axis=-1, keepdims=True) + norm_eps)
    return (center * inverse, inverse)


def norm_back(grad_hat, normed, inverse):
    first_mean = jnp.mean(grad_hat, axis=-1, keepdims=True)
    cross_mean = jnp.mean(grad_hat * normed, axis=-1, keepdims=True)
    return (grad_hat - first_mean - normed * cross_mean) * inverse


def rotary_tables(pos_row):
    half_dim = HD // 2
    frequency = rope_base ** (-(jnp.arange(half_dim).astype(jnp.float32) * (2.0 / HD)))
    angles = pos_row.astype(jnp.float32)[:, None] * frequency[None, :]
    return (jnp.cos(angles)[:, None, :], jnp.sin(angles)[:, None, :])


def rotate(matrix, cosine, sine_part):
    half_dim = HD // 2
    first_half = matrix[..., :half_dim]
    second_half = matrix[..., half_dim:]
    return jnp.concatenate(
        [
            first_half * cosine - second_half * sine_part,
            second_half * cosine + first_half * sine_part,
        ],
        axis=-1,
    )


def unrotate(matrix, cosine, sine_part):
    half_dim = HD // 2
    first_half = matrix[..., :half_dim]
    second_half = matrix[..., half_dim:]
    return jnp.concatenate(
        [
            first_half * cosine + second_half * sine_part,
            second_half * cosine - first_half * sine_part,
        ],
        axis=-1,
    )


def gelu_pair(gate_half):
    normal_cdf = 0.5 * (1.0 + lax.erf(gate_half * 0.7071067811865476))
    density = jnp.exp(-0.5 * gate_half * gate_half) * 0.3989422804014327
    return (gate_half * normal_cdf, normal_cdf + gate_half * density)


def forward_dot(left, right):
    return jnp.dot(left, right, preferred_element_type=jnp.float32)


def against_rows(left, right):
    return lax.dot_general(
        left, right, (((1,), (1,)), ((), ())), preferred_element_type=jnp.float32
    )


def over_rows(left, right):
    return lax.dot_general(
        left, right, (((0,), (0,)), ((), ())), preferred_element_type=jnp.float32
    )


def fetch_forward(w_qkv, w_out, w_in, w_down, gain_attn, gain_ffn):
    return in_one_piece((w_qkv, w_out, w_in, w_down, gain_attn, gain_ffn), ("dp", "seq"), 0, 1)


def owner_order(matrix, dp_count, seq_count):
    row_count = matrix.shape[0]
    share = matrix.shape[1] // (dp_count * seq_count)
    return (
        matrix.reshape(row_count, dp_count, seq_count, share)
        .transpose(0, 2, 1, 3)
        .reshape(row_count, matrix.shape[1])
    )


def body(
    block_input, doc_ids, positions, w_qkv, w_out, w_in, w_down, gain_attn, gain_ffn, cotangent
):
    rows_here = block_input.shape[1]
    seq_len = doc_ids.shape[1]
    dp_count = lax.axis_size("dp")
    seq_count = lax.axis_size("seq")
    owned_rows = w_qkv.shape[0]
    local_rows = owned_rows * dp_count
    offset = lax.axis_index("seq") * rows_here
    score_scale = HD ** (-0.5)
    running = (
        jnp.zeros((local_rows, 3 * D), jnp.float32),
        jnp.zeros((local_rows, D), jnp.float32),
        jnp.zeros((local_rows, 2 * FF), jnp.float32),
        jnp.zeros((local_rows, FF), jnp.float32),
    )
    gain_running = (jnp.zeros((D,), jnp.float32), jnp.zeros((D,), jnp.float32))
    own_parts = (
        jnp.zeros(w_qkv.shape, jnp.float32),
        jnp.zeros(w_out.shape, jnp.float32),
        jnp.zeros(w_in.shape, jnp.float32),
        jnp.zeros(w_down.shape, jnp.float32),
    )
    gain_parts = (jnp.zeros(gain_attn.shape, jnp.float32), jnp.zeros(gain_ffn.shape, jnp.float32))
    outputs = []
    input_grads = []
    for step_index in range(block_input.shape[0]):
        whole = fetch_forward(w_qkv, w_out, w_in, w_down, gain_attn, gain_ffn)
        fwd_qkv, fwd_out, fwd_in, fwd_down, fwd_gain_attn, fwd_gain_ffn = whole
        tokens = block_input[step_index]
        grad_top = cotangent[step_index]
        doc_row = doc_ids[step_index]
        doc_here = lax.dynamic_slice_in_dim(doc_row, offset, rows_here)
        cosine, sine_part = rotary_tables(positions[step_index])
        normed_one, inverse_one = normalize(tokens)
        input_one = (normed_one * fwd_gain_attn.astype(jnp.float32)).astype(jnp.bfloat16)
        packed = forward_dot(input_one, fwd_qkv)
        queries = rotate(packed[:, :D].reshape(rows_here, H, HD), cosine, sine_part).astype(
            jnp.bfloat16
        )
        key_here = (
            rotate(packed[:, D : 2 * D].reshape(rows_here, H, HD), cosine, sine_part)
            .astype(jnp.bfloat16)
            .reshape(rows_here, D)
        )
        value_here = packed[:, 2 * D :].astype(jnp.bfloat16)
        key_all, value_all = (
            lax.all_gather(key_here, "seq", axis=0, tiled=True),
            lax.all_gather(value_here, "seq", axis=0, tiled=True),
        )
        key_heads = key_all.reshape(seq_len, H, HD)
        value_heads = value_all.reshape(seq_len, H, HD)
        same_doc = (doc_here[:, None] == doc_row[None, :])[None]
        scores = (
            jnp.einsum("qhd,khd->hqk", queries, key_heads, preferred_element_type=jnp.float32)
            * score_scale
        )
        masked = jnp.where(same_doc, scores, -jnp.inf)
        row_top = jnp.max(masked, axis=-1, keepdims=True)
        log_total = row_top + jnp.log(jnp.sum(jnp.exp(masked - row_top), axis=-1, keepdims=True))
        soft_low = jnp.exp(masked - log_total).astype(jnp.bfloat16)
        attended = (
            jnp.einsum("hqk,khd->qhd", soft_low, value_heads, preferred_element_type=jnp.float32)
            .reshape(rows_here, D)
            .astype(jnp.bfloat16)
        )
        residual = tokens + against_rows(attended, fwd_out)
        normed_two, inverse_two = normalize(residual)
        input_two = (normed_two * fwd_gain_ffn.astype(jnp.float32)).astype(jnp.bfloat16)
        pre_act = forward_dot(input_two, fwd_in)
        gate_half = pre_act[:, :FF]
        up_half = pre_act[:, FF:]
        activated, gate_slope = gelu_pair(gate_half)
        hidden = (activated * up_half).astype(jnp.bfloat16)
        outputs.append(residual + against_rows(hidden, fwd_down))
        back_qkv, back_out, back_in, back_down, back_gain_attn, back_gain_ffn = whole
        grad_low = grad_top.astype(jnp.bfloat16)
        grad_hidden = forward_dot(grad_low, back_down)
        grad_pre = jnp.concatenate(
            [grad_hidden * up_half * gate_slope, grad_hidden * activated], axis=-1
        ).astype(jnp.bfloat16)
        grad_norm_two = against_rows(grad_pre, back_in)
        grad_gain_ffn = jnp.sum(grad_norm_two * normed_two, axis=0)
        grad_resid = grad_top + norm_back(
            grad_norm_two * back_gain_ffn.astype(jnp.float32), normed_two, inverse_two
        )
        resid_low = grad_resid.astype(jnp.bfloat16)
        grad_att = forward_dot(resid_low, back_out).astype(jnp.bfloat16).reshape(rows_here, H, HD)
        row_delta = jnp.sum(
            grad_att.astype(jnp.float32) * attended.reshape(rows_here, H, HD).astype(jnp.float32),
            axis=-1,
        ).T[:, :, None]
        scores_again = (
            jnp.einsum("qhd,khd->hqk", queries, key_heads, preferred_element_type=jnp.float32)
            * score_scale
        )
        soft_again = jnp.exp(jnp.where(same_doc, scores_again, -jnp.inf) - log_total)
        grad_probs = jnp.einsum(
            "qhd,khd->hqk", grad_att, value_heads, preferred_element_type=jnp.float32
        )
        grad_scores = (soft_again * (grad_probs - row_delta) * score_scale).astype(jnp.bfloat16)
        grad_query = jnp.einsum(
            "hqk,khd->qhd", grad_scores, key_heads, preferred_element_type=jnp.float32
        )
        grad_key_all = jnp.einsum(
            "hqk,qhd->khd", grad_scores, queries, preferred_element_type=jnp.float32
        ).reshape(seq_len, D)
        grad_value_all = jnp.einsum(
            "hqk,qhd->khd", soft_low, grad_att, preferred_element_type=jnp.float32
        ).reshape(seq_len, D)
        grad_key_here, grad_value_here = sent_together((grad_key_all, grad_value_all), "seq", 0, 1)
        grad_packed = jnp.concatenate(
            [
                unrotate(grad_query, cosine, sine_part).reshape(rows_here, D),
                unrotate(grad_key_here.reshape(rows_here, H, HD), cosine, sine_part).reshape(
                    rows_here, D
                ),
                grad_value_here,
            ],
            axis=-1,
        ).astype(jnp.bfloat16)
        grad_norm_one = against_rows(grad_packed, back_qkv)
        grad_gain_attn = jnp.sum(grad_norm_one * normed_one, axis=0)
        input_grads.append(
            grad_resid
            + norm_back(grad_norm_one * back_gain_attn.astype(jnp.float32), normed_one, inverse_one)
        )
        row_one, row_two, row_resid, row_grad = (
            lax.all_to_all(
                owner_order(input_one, dp_count, seq_count),
                "seq",
                split_axis=1,
                concat_axis=0,
                tiled=True,
            ),
            lax.all_to_all(
                owner_order(input_two, dp_count, seq_count),
                "seq",
                split_axis=1,
                concat_axis=0,
                tiled=True,
            ),
            lax.all_to_all(
                owner_order(resid_low, dp_count, seq_count),
                "seq",
                split_axis=1,
                concat_axis=0,
                tiled=True,
            ),
            lax.all_to_all(
                owner_order(grad_low, dp_count, seq_count),
                "seq",
                split_axis=1,
                concat_axis=0,
                tiled=True,
            ),
        )
        packed_seq, pre_seq, attended_seq, hidden_seq = side_by_side(
            (grad_packed, grad_pre, attended, hidden), "seq", 0, 1
        )
        terms = (
            over_rows(row_one, packed_seq),
            over_rows(row_resid, attended_seq),
            over_rows(row_two, pre_seq),
            over_rows(row_grad, hidden_seq),
        )
        gain_terms = (grad_gain_attn, grad_gain_ffn)
        running = jax.tree.map(jnp.add, running, terms)
        gain_running = jax.tree.map(jnp.add, gain_running, gain_terms)
    own_parts = in_one_piece_2((running[0], running[1], running[2], running[3]), "dp", 0, 1)
    gain_parts = (
        lax.psum_scatter(gain_running[0], ("dp", "seq"), scatter_dimension=0, tiled=True),
        lax.psum_scatter(gain_running[1], ("dp", "seq"), scatter_dimension=0, tiled=True),
    )
    return (
        jnp.stack(outputs),
        jnp.stack(input_grads),
        own_parts[0],
        own_parts[1],
        own_parts[2],
        own_parts[3],
        gain_parts[0],
        gain_parts[1],
    )


def solution(mesh):
    return jax.shard_map(
        body,
        mesh=mesh,
        in_specs=(
            P("dp", "seq", None),
            P("dp", None),
            P("dp", "seq"),
            P(("dp", "seq"), None),
            P(("dp", "seq"), None),
            P(("dp", "seq"), None),
            P(("dp", "seq"), None),
            P(("dp", "seq")),
            P(("dp", "seq")),
            P("dp", "seq", None),
        ),
        out_specs=(
            P("dp", "seq", None),
            P("dp", "seq", None),
            P(("dp", "seq"), None),
            P(("dp", "seq"), None),
            P(("dp", "seq"), None),
            P(("dp", "seq"), None),
            P(("dp", "seq")),
            P(("dp", "seq")),
        ),
        check_vma=False,
    )
```

profile of v0, /device:TPU:1, one launch (start us, length us, event | category | flops | bytes accessed | tf_op | source)
XLA Modules:
  0.0 1065.7 jit_solution(9702997083633565786)
XLA Ops:
  16.4 425.0 %all-gather.9.cloned.1.call-done = bf16[256,3,6530]{2,1,0:T(4,128)(2,1)} async-done(((bf16[1,3,6530]{2,1,0:T(4,128)(2,1)}), bf16[256,3,6530]{2,1,0:T(4,128)(2,1)}) %all-gather.9.cloned.1.call-update) | async-done | bytes 10030096 | tf_op jit(solution)/shard_map/all_gather | solution.py:20
  441.4 24.2 %reshape.524 = bf16[768,6530]{1,0:T(8,128)(2,1)} reshape(bf16[256,3,6530]{2,1,0:T(4,128)(2,1)} %all-gather.9.cloned.1.call-done) | data formatting | bytes 20060160
  474.9 12.1 %all_gather.26 = bf16[512,768]{0,1:T(8,128)(2,1)} all-gather(bf16[128,768]{0,1:T(8,128)(2,1)S(1)} %bitcast.287), channel_id=1, replica_groups=mesh['dp'=64,'seq'=4] {'seq'}, dimensions={0}, use_global_device_ids=true | all-gather | bytes 983040 | tf_op jit(solution)/shard_map/all_gather | solution.py:195
  487.1 10.2 all_gather.25
  499.6 10.4 all_gather.24
  510.0 11.6 %all_gather.23 = bf16[512,768]{1,0:T(8,128)(2,1)} all-gather(bf16[128,768]{1,0:T(8,128)(2,1)} %slice.321), channel_id=1, replica_groups=mesh['dp'=64,'seq'=4] {'seq'}, dimensions={0}, use_global_device_ids=true | all-gather | bytes 983040 | tf_op jit(solution)/shard_map/all_gather | solution.py:196
  547.6 4.1 fusion.104
  558.2 3.4 pad_maximum_fusion.1
  585.2 21.6 %reduce-scatter.3.cloned.1.call-done = f32[128,1536]{1,0:T(8,128)} async-done(((f32[512,1536]{1,0:T(8,128)}), f32[128,1536]{1,0:T(8,128)}) %reduce-scatter.3.cloned.1.call-update) | async-done | bytes 786448 | tf_op jit(solution)/shard_map/reduce_scatter | solution.py:34
  619.7 39.6 %reduce-scatter.5.cloned.1.call-done = f32[128,1536]{1,0:T(8,128)} async-done(((f32[512,1536]{1,0:T(8,128)}), f32[128,1536]{1,0:T(8,128)}) %reduce-scatter.5.cloned.1.call-update) | async-done | bytes 786448 | tf_op jit(solution)/shard_map/reduce_scatter | solution.py:34
  678.5 4.2 all-to-all-start.4
  691.1 4.2 all-to-all-start.5
  695.3 25.1 %all-gather.5.cloned.1.call-done = bf16[512,6528]{1,0:T(8,128)(2,1)} async-done(((bf16[128,6528]{1,0:T(8,128)(2,1)}), bf16[512,6528]{1,0:T(8,128)(2,1)}) %all-gather.5.cloned.1.call-update) | async-done | bytes 6684688 | tf_op jit(solution)/shard_map/all_gather | solution.py:40
  720.3 3.6 fusion.4
  723.9 3.6 all-to-all-start
  727.5 49.2 %all-gather.7.cloned.1.call-done = bf16[512,6528]{1,0:T(8,128)(2,1)} async-done(((bf16[128,6528]{1,0:T(8,128)(2,1)}), bf16[512,6528]{1,0:T(8,128)(2,1)}) %all-gather.7.cloned.1.call-update) | async-done | bytes 6684688 | tf_op jit(solution)/shard_map/all_gather | solution.py:40
  779.5 3.6 all-to-all-start.6
  783.1 3.6 fusion.7
  789.1 4.2 all-to-all-start.7
  795.9 3.3 all-to-all-done.7
  799.9 4.2 all-to-all-start.2
  806.2 4.0 all-to-all-done.2
  810.1 4.8 all-to-all-start.3
  817.2 3.8 all-to-all-done.3
  821.0 4.2 all-to-all-start.1
  827.7 3.5 all-to-all-done.1
  836.6 8.0 reshape.519
  844.7 10.6 all-to-all-start.8
  855.3 3.4 fusion.17
  858.8 4.7 multiply_reduce_fusion.3
  863.5 181.9 %all-reduce.2 = (f32[768]{0:T(1024)S(1)}, f32[768]{0:T(1024)S(1)}) all-reduce(f32[768]{0:T(1024)S(1)} %add.173, f32[768]{0:T(1024)S(1)} %add.174), channel_id=4, replica_groups=mesh['dp'=64,'seq'=4] {'dp','seq'}, use_global_device_ids=true, to_apply=%region_27.28.clone | all-reduce | flops 1536 | bytes 12288
  1053.3 3.8 reduce_sum.245
  (383 shorter events, 146.5 us)
Async XLA Ops:
  7.2 434.2 %all-gather.9.cloned.1.call-start = ((), (), s32[]{:S(2)}) async-start(), calls=%async_computation.15 | async-start | bytes 13684736 | tf_op jit(solution)/shard_map/all_gather | solution.py:20
  10.2 596.6 %reduce-scatter.3.cloned.1.call-start = ((), (), s32[]{:S(2)}) async-start(), calls=%async_computation.11 | async-start | bytes 3932160 | tf_op jit(solution)/shard_map/reduce_scatter | solution.py:34
  13.1 454.4 %copy-start.81 = (f32[128]{0:T(128)}, f32[128]{0:T(128)S(1)}, u32[]{:S(2)}) copy-start(f32[128]{0:T(128)S(1)} %get-tuple-element.108) | copy-start | bytes 1540
  13.1 457.2 %copy-start.83 = (f32[128]{0:T(128)}, f32[128]{0:T(128)S(1)}, u32[]{:S(2)}) copy-start(f32[128]{0:T(128)S(1)} %get-tuple-element.109) | copy-start | bytes 1540
  14.5 455.8 %copy-start.87 = (f32[128]{0:T(128)}, f32[128]{0:T(128)S(1)}, u32[]{:S(2)}) copy-start(f32[128]{0:T(128)S(1)} %add_rsqrt_fusion.3) | copy-start | bytes 1540
  14.5 453.0 %copy-start.89 = (f32[128]{0:T(128)}, f32[128]{0:T(128)S(1)}, u32[]{:S(2)}) copy-start(f32[128]{0:T(128)S(1)} %add_rsqrt_fusion.1) | copy-start | bytes 1540
  15.5 458.6 %copy-start.70 = (f32[128,32]{0,1:T(8,128)}, f32[128,32]{0,1:T(8,128)S(1)}, u32[]{:S(2)}) copy-start(f32[128,32]{0,1:T(8,128)S(1)} %get-tuple-element.96) | copy-start | bytes 49156
  15.5 483.2 %copy-start.71 = (f32[128,32]{0,1:T(8,128)}, f32[128,32]{0,1:T(8,128)S(1)}, u32[]{:S(2)}) copy-start(f32[128,32]{0,1:T(8,128)S(1)} %get-tuple-element.89) | copy-start | bytes 49156
  15.5 483.2 %copy-start.73 = (f32[128,32]{0,1:T(8,128)}, f32[128,32]{0,1:T(8,128)S(1)}, u32[]{:S(2)}) copy-start(f32[128,32]{0,1:T(8,128)S(1)} %get-tuple-element.90) | copy-start | bytes 49156
  16.4 510.2 %copy-start.38 = (pred[128,512]{1,0:T(8,128)(4,1)}, pred[128,512]{1,0:T(8,128)(4,1)S(1)}, u32[]{:S(2)}) copy-start(pred[128,512]{1,0:T(8,128)(4,1)S(1)} %broadcast_compare_fusion.1) | copy-start | bytes 196612
  16.4 451.1 %copy-start.4 = (f32[2,128,768]{2,1,0:T(8,128)S(1)}, f32[2,128,768]{2,1,0:T(8,128)}, u32[]{:S(2)}) copy-start(f32[2,128,768]{2,1,0:T(8,128)} %param.10) | copy-start | bytes 2359300
  499.6 30.8 %slice-start = ((s8[10223616]{0:T(1024)(128)(4,1)}), s8[1835008]{0:T(1024)(128)(4,1)S(1)}, s32[]{:S(2)}) async-start(s8[10223616]{0:T(1024)(128)(4,1)} %bitcast.239), calls=%async_computation.16 | async-start | bytes 3670016
  510.0 15.7 %copy-start.8 = (bf16[512,768]{0,1:T(8,128)(2,1)}, bf16[512,768]{0,1:T(8,128)(2,1)S(1)}, u32[]{:S(2)}) copy-start(bf16[512,768]{0,1:T(8,128)(2,1)S(1)} %all_gather.24) | copy-start | bytes 2359300
  561.6 97.7 %reduce-scatter.5.cloned.1.call-start = ((), (), s32[]{:S(2)}) async-start(), calls=%async_computation.12 | async-start | bytes 3932160 | tf_op jit(solution)/shard_map/reduce_scatter | solution.py:34
  582.8 25.2 %copy-start.72 = (f32[128,32]{0,1:T(8,128)S(1)}, f32[128,32]{0,1:T(8,128)}, u32[]{:S(2)}) copy-start(f32[128,32]{0,1:T(8,128)} %copy-done.71) | copy-start | bytes 49156
  582.8 25.2 %copy-start.74 = (f32[128,32]{0,1:T(8,128)S(1)}, f32[128,32]{0,1:T(8,128)}, u32[]{:S(2)}) copy-start(f32[128,32]{0,1:T(8,128)} %copy-done.73) | copy-start | bytes 49156
  582.8 137.5 %all-gather.5.cloned.1.call-start = ((), (), s32[]{:S(2)}) async-start(), calls=%async_computation.13 | async-start | bytes 8355840 | tf_op jit(solution)/shard_map/all_gather | solution.py:40
  618.2 158.5 %all-gather.7.cloned.1.call-start = ((), (), s32[]{:S(2)}) async-start(), calls=%async_computation.14 | async-start | bytes 8355840 | tf_op jit(solution)/shard_map/all_gather | solution.py:40
  678.5 12.6 %all-to-all-start.4 = ((bf16[128,4,192]{0,2,1:T(8,128)(2,1)}), bf16[128,4,192]{0,2,1:T(8,128)(2,1)S(1)}, u32[]{:S(2)}, u32[]{:S(2)}) async-start(bf16[128,4,192]{0,2,1:T(8,128)(2,1)} %copy.141), calls=%async_computation.6 | async-start | bytes 393216 | tf_op jit(solution)/shard_map/all_to_all | solution.py:283
  691.1 32.8 %all-to-all-start.5 = ((bf16[128,4,192]{0,2,1:T(8,128)(2,1)}), bf16[128,4,192]{0,2,1:T(8,128)(2,1)S(1)}, u32[]{:S(2)}, u32[]{:S(2)}) async-start(bf16[128,4,192]{0,2,1:T(8,128)(2,1)} %copy.145), calls=%async_computation.7 | async-start | bytes 393216 | tf_op jit(solution)/shard_map/all_to_all | solution.py:283
  723.9 55.6 %all-to-all-start = ((bf16[128,4,192]{0,2,1:T(8,128)(2,1)}), bf16[128,4,192]{0,2,1:T(8,128)(2,1)S(1)}, u32[]{:S(2)}, u32[]{:S(2)}) async-start(bf16[128,4,192]{0,2,1:T(8,128)(2,1)} %copy.119), calls=%async_computation.2 | async-start | bytes 393216 | tf_op jit(solution)/shard_map/all_to_all | solution.py:276
  779.5 9.6 all-to-all-start.6
  789.1 10.2 all-to-all-start.7
  799.9 10.2 all-to-all-start.2
  810.1 10.9 %all-to-all-start.3 = ((bf16[128,4,192]{0,2,1:T(8,128)(2,1)}), bf16[128,4,192]{0,2,1:T(8,128)(2,1)}, u32[]{:S(2)}, u32[]{:S(2)}) async-start(bf16[128,4,192]{0,2,1:T(8,128)(2,1)} %copy.137), calls=%async_computation.5 | async-start | bytes 393216 | tf_op jit(solution)/shard_map/all_to_all | solution.py:290
  821.0 10.2 all-to-all-start.1
  844.6 10.6 copy-start.59
  844.6 10.6 copy-start.60
  844.6 10.6 copy-start.69
  844.7 208.6 %all-to-all-start.8 = ((f32[64,3,6528]{2,1,0:T(4,128)}), f32[64,3,6528]{2,1,0:T(4,128)}, u32[]{:S(2)}, u32[]{:S(2)}) async-start(f32[64,3,6528]{2,1,0:T(4,128)} %reshape.519), calls=%async_computation.10 | async-start | bytes 13369344 | tf_op jit(solution)/shard_map/all_to_all | solution.py:55
  858.8 190.1 %copy-start.12 = (f32[128,768]{1,0:T(8,128)S(1)}, f32[128,768]{1,0:T(8,128)}, u32[]{:S(2)}) copy-start(f32[128,768]{1,0:T(8,128)} %copy-done.11) | copy-start | bytes 1179652
  858.8 190.1 %copy-start.36 = (bf16[128,1152]{1,0:T(8,128)(2,1)S(1)}, bf16[128,1152]{1,0:T(8,128)(2,1)}, u32[]{:S(2)}) copy-start(bf16[128,1152]{1,0:T(8,128)(2,1)} %get-tuple-element.31) | copy-start | bytes 884740
  (82 other events, 327.8 us)
Sparse Core Ops, SparseCore 0:
  10.5 430.8 all-gather.8
  561.7 45.0 reduce-scatter.2
  609.8 49.4 reduce-scatter.4
  661.0 59.2 all-gather.4
  722.0 54.6 all-gather.6
where the time goes:
time: 1070 us
  waiting for transfers between devices  580 us (54%)
  blocking collectives  226 us (21%)
  local copies, waits for them, and re-layouts  93.9 us (9%)
  matrix products  71.9 us (7%)
  starting transfers between devices  43.7 us (4%)
  other arithmetic  34.1 us (3%)
  between operations  15.7 us (1%)
    all_gather x1, waiting for transfers between devices, in_one_piece(): filled = lax.all_gather(both, axis, axis=dim, tiled=True)  425 us
    unnamed x1, blocking collectives  182 us
    all_gather x2, waiting for transfers between devices, side_by_side(): filled, at, done = (lax.all_gather(both, axis, axis=dim, tiled=True), 0, [])  74.2 us
    reduce_scatter x2, waiting for transfers between devices, sent_together(): lax.psum_scatter(both, axis, scatter_dimension=dim, tiled=True)  61.2 us
    unnamed x215, local copies, waits for them, and re-layouts  47.2 us
    all_gather x2, blocking collectives, body(): lax.all_gather(key_here, 'seq', axis=0, tiled=True)  22.5 us
    dot_general x8, matrix products, over_rows(): lax.dot_general(left, right, (((0,), (0,)), ((), ())), preferred_element_...  22.3 us
    all_gather x2, blocking collectives, body(): lax.all_gather(value_here, 'seq', axis=0, tiled=True)  21.8 us
  transfers between devices with their start and end apart: 14, of which 11 were waited for; matrix products, arithmetic and copies ran while one was open for 9% of the time, Pallas kernels for 0%

commit v1 on v0

--- a/solution.py
+++ b/solution.py
@@ -193,7 +193,9 @@
         value_here = packed[:, 2 * D :].astype(jnp.bfloat16)
         key_all, value_all = (
             lax.all_gather(key_here, "seq", axis=0, tiled=True),
-            lax.all_gather(value_here, "seq", axis=0, tiled=True),
+            jnp.concatenate(
+                lax.all_to_all(jnp.stack([value_here] * lax.axis_size("seq")), "seq", 0, 0), axis=0
+            ),
         )
         key_heads = key_all.reshape(seq_len, H, HD)
         value_heads = value_all.reshape(seq_len, H, HD)

time: 1070 us -> 1090 us (1.019)
  blocking collectives: 226 us -> 209 us
  starting transfers between devices: 43.7 us -> 55.4 us
    all_gather x2 -> x0, blocking collectives: 21.8 us -> none  [body(): lax.all_gather(value_here, 'seq', axis=0, tiled=True)]
    all_to_all x0 -> x2, starting transfers between devices: none -> 11.6 us  [body(): lax.all_to_all(jnp.stack([value_here] * lax.axis_size('seq')), 'seq', 0, 0)]
    unnamed x215 -> x223, local copies, waits for them, and re-layouts: 47.2 us -> 49.5 us
  transfers between devices with their start and end apart: 14 -> 16, of which waited for: 11 -> 12; matrix products, arithmetic and copies ran while one was open for 9% -> 10% of each run, Pallas kernels for 0% -> 0%
where the time goes in v1:
time: 1090 us; the launch traced here: 1080 us
  waiting for transfers between devices  588 us (54%)
  blocking collectives  209 us (19%)
  local copies, waits for them, and re-layouts  104 us (10%)
  matrix products  74.5 us (7%)
  starting transfers between devices  55.4 us (5%)
  other arithmetic  31.8 us (3%)
  between operations  15.8 us (1%)
    all_gather x1, waiting for transfers between devices, in_one_piece(): filled = lax.all_gather(both, axis, axis=dim, tiled=True)  426 us
    unnamed x1, blocking collectives  182 us
    all_gather x2, waiting for transfers between devices, side_by_side(): filled, at, done = (lax.all_gather(both, axis, axis=dim, tiled=True), 0, [])  75.6 us
    reduce_scatter x2, waiting for transfers between devices, sent_together(): lax.psum_scatter(both, axis, scatter_dimension=dim, tiled=True)  60.8 us
    unnamed x223, local copies, waits for them, and re-layouts  49.5 us
    all_gather x2, blocking collectives, body(): lax.all_gather(key_here, 'seq', axis=0, tiled=True)  27 us
    dot_general x8, matrix products, over_rows(): lax.dot_general(left, right, (((0,), (0,)), ((), ())), preferred_element_...  22.3 us
  transfers between devices with their start and end apart: 16, of which 12 were waited for; matrix products, arithmetic and copies ran while one was open for 10% of the time, Pallas kernels for 0%

profile of v1, /device:TPU:1, one launch (start us, length us, event | category | flops | bytes accessed | tf_op | source)
XLA Modules:
  0.0 1077.9 jit_solution(15295854174318778108)
XLA Ops:
  15.8 425.6 %all-gather.9.cloned.1.call-done = bf16[256,3,6530]{2,1,0:T(4,128)(2,1)} async-done(((bf16[1,3,6530]{2,1,0:T(4,128)(2,1)}), bf16[256,3,6530]{2,1,0:T(4,128)(2,1)}) %all-gather.9.cloned.1.call-update) | async-done | bytes 10030096 | tf_op jit(solution)/shard_map/all_gather | solution.py:20
  441.4 24.3 %reshape.520 = bf16[768,6530]{1,0:T(8,128)(2,1)} reshape(bf16[256,3,6530]{2,1,0:T(4,128)(2,1)} %all-gather.9.cloned.1.call-done) | data formatting | bytes 20060160
  474.6 7.2 all-to-all-start.1
  483.2 16.8 %all_gather.17 = bf16[512,768]{0,1:T(8,128)(2,1)S(1)} all-gather(bf16[128,768]{0,1:T(8,128)(2,1)S(1)} %bitcast.286), channel_id=1, replica_groups=mesh['dp'=64,'seq'=4] {'seq'}, dimensions={0}, use_global_device_ids=true | all-gather | bytes 983040 | tf_op jit(solution)/shard_map/all_gather | solution.py:195
  502.5 10.2 all_gather.18
  516.6 4.3 all-to-all-start
  527.9 5.5 all-to-all-done
  560.2 4.1 fusion.104
  570.6 3.4 pad_maximum_fusion.1
  597.6 21.2 %reduce-scatter.3.cloned.1.call-done = f32[128,1536]{1,0:T(8,128)} async-done(((f32[512,1536]{1,0:T(8,128)}), f32[128,1536]{1,0:T(8,128)}) %reduce-scatter.3.cloned.1.call-update) | async-done | bytes 786448 | tf_op jit(solution)/shard_map/reduce_scatter | solution.py:34
  631.7 39.6 %reduce-scatter.5.cloned.1.call-done = f32[128,1536]{1,0:T(8,128)} async-done(((f32[512,1536]{1,0:T(8,128)}), f32[128,1536]{1,0:T(8,128)}) %reduce-scatter.5.cloned.1.call-update) | async-done | bytes 786448 | tf_op jit(solution)/shard_map/reduce_scatter | solution.py:34
  689.3 4.0 all-to-all-start.6
  701.8 4.2 all-to-all-start.7
  705.9 26.4 %all-gather.5.cloned.1.call-done = bf16[512,6528]{1,0:T(8,128)(2,1)} async-done(((bf16[128,6528]{1,0:T(8,128)(2,1)}), bf16[512,6528]{1,0:T(8,128)(2,1)}) %all-gather.5.cloned.1.call-update) | async-done | bytes 6684688 | tf_op jit(solution)/shard_map/all_gather | solution.py:40
  732.3 3.6 fusion.4
  735.9 3.6 all-to-all-start.2
  739.5 49.2 %all-gather.7.cloned.1.call-done = bf16[512,6528]{1,0:T(8,128)(2,1)} async-done(((bf16[128,6528]{1,0:T(8,128)(2,1)}), bf16[512,6528]{1,0:T(8,128)(2,1)}) %all-gather.7.cloned.1.call-update) | async-done | bytes 6684688 | tf_op jit(solution)/shard_map/all_gather | solution.py:40
  791.5 3.6 all-to-all-start.8
  795.1 3.6 fusion.7
  801.1 4.4 all-to-all-start.9
  812.1 4.2 all-to-all-start.4
  818.3 4.0 all-to-all-done.4
  822.3 4.8 all-to-all-start.5
  829.4 3.8 all-to-all-done.5
  833.2 4.2 all-to-all-start.3
  839.9 3.5 all-to-all-done.3
  848.8 8.0 reshape.515
  856.9 10.6 all-to-all-start.10
  867.6 3.4 fusion.17
  871.0 4.7 multiply_reduce_fusion.3
  875.7 181.9 %all-reduce.2 = (f32[768]{0:T(1024)S(1)}, f32[768]{0:T(1024)S(1)}) all-reduce(f32[768]{0:T(1024)S(1)} %add.173, f32[768]{0:T(1024)S(1)} %add.174), channel_id=4, replica_groups=mesh['dp'=64,'seq'=4] {'dp','seq'}, use_global_device_ids=true, to_apply=%region_27.28.clone | all-reduce | flops 1536 | bytes 12288
  1065.5 3.8 reduce_sum.245
  (399 shorter events, 160.7 us)
Async XLA Ops:
  7.2 434.2 %all-gather.9.cloned.1.call-start = ((), (), s32[]{:S(2)}) async-start(), calls=%async_computation.17 | async-start | bytes 13684736 | tf_op jit(solution)/shard_map/all_gather | solution.py:20
  13.1 454.4 %copy-start.85 = (f32[128]{0:T(128)}, f32[128]{0:T(128)S(1)}, u32[]{:S(2)}) copy-start(f32[128]{0:T(128)S(1)} %get-tuple-element.108) | copy-start | bytes 1540
  13.1 457.2 %copy-start.87 = (f32[128]{0:T(128)}, f32[128]{0:T(128)S(1)}, u32[]{:S(2)}) copy-start(f32[128]{0:T(128)S(1)} %get-tuple-element.109) | copy-start | bytes 1540
  14.5 455.9 %copy-start.91 = (f32[128]{0:T(128)}, f32[128]{0:T(128)S(1)}, u32[]{:S(2)}) copy-start(f32[128]{0:T(128)S(1)} %add_rsqrt_fusion.3) | copy-start | bytes 1540
  14.5 453.0 %copy-start.93 = (f32[128]{0:T(128)}, f32[128]{0:T(128)S(1)}, u32[]{:S(2)}) copy-start(f32[128]{0:T(128)S(1)} %add_rsqrt_fusion.1) | copy-start | bytes 1540
  15.5 467.5 %copy-start.75 = (f32[128,32]{0,1:T(8,128)}, f32[128,32]{0,1:T(8,128)S(1)}, u32[]{:S(2)}) copy-start(f32[128,32]{0,1:T(8,128)S(1)} %get-tuple-element.89) | copy-start | bytes 49156
  15.5 467.5 %copy-start.77 = (f32[128,32]{0,1:T(8,128)}, f32[128,32]{0,1:T(8,128)S(1)}, u32[]{:S(2)}) copy-start(f32[128,32]{0,1:T(8,128)S(1)} %get-tuple-element.90) | copy-start | bytes 49156
  15.5 484.5 %copy-start.74 = (f32[128,32]{0,1:T(8,128)}, f32[128,32]{0,1:T(8,128)S(1)}, u32[]{:S(2)}) copy-start(f32[128,32]{0,1:T(8,128)S(1)} %get-tuple-element.96) | copy-start | bytes 49156
  15.6 505.3 %copy-start.39 = (pred[128,512]{1,0:T(8,128)(4,1)}, pred[128,512]{1,0:T(8,128)(4,1)S(1)}, u32[]{:S(2)}) copy-start(pred[128,512]{1,0:T(8,128)(4,1)S(1)} %broadcast_compare_fusion) | copy-start | bytes 196612
  15.7 520.5 %copy-start.41 = (pred[128,512]{1,0:T(8,128)(4,1)}, pred[128,512]{1,0:T(8,128)(4,1)S(1)}, u32[]{:S(2)}) copy-start(pred[128,512]{1,0:T(8,128)(4,1)S(1)} %broadcast_compare_fusion.1) | copy-start | bytes 196612
  15.8 451.8 %copy-start.5 = (f32[2,128,768]{2,1,0:T(8,128)S(1)}, f32[2,128,768]{2,1,0:T(8,128)}, u32[]{:S(2)}) copy-start(f32[2,128,768]{2,1,0:T(8,128)} %param.10) | copy-start | bytes 2359300
  474.6 39.8 %all-to-all-start.1 = ((bf16[4,128,768]{1,2,0:T(8,128)(2,1)}), bf16[4,128,768]{1,2,0:T(8,128)(2,1)}, u32[]{:S(2)}, u32[]{:S(2)}) async-start(bf16[4,128,768]{1,2,0:T(8,128)(2,1)} %stack.34), calls=%async_computation.1 | async-start | bytes 1572864 | tf_op jit(solution)/shard_map/all_to_all | solution.py:197
  483.1 18.5 %copy-start.47 = (bf16[128,12,32]{0,2,1:T(8,128)(2,1)}, bf16[128,12,32]{0,2,1:T(8,128)(2,1)S(1)}, u32[]{:S(2)}) copy-start(bf16[128,12,32]{0,2,1:T(8,128)(2,1)S(1)} %get-tuple-element.62) | copy-start | bytes 294916
  483.1 18.5 %copy-start.49 = (bf16[128,12,32]{0,2,1:T(8,128)(2,1)}, bf16[128,12,32]{0,2,1:T(8,128)(2,1)S(1)}, u32[]{:S(2)}) copy-start(bf16[128,12,32]{0,2,1:T(8,128)(2,1)S(1)} %get-tuple-element.63) | copy-start | bytes 294916
  516.6 16.7 %all-to-all-start = ((bf16[4,128,768]{1,2,0:T(8,128)(2,1)}), bf16[4,128,768]{1,2,0:T(8,128)(2,1)}, u32[]{:S(2)}, u32[]{:S(2)}) async-start(bf16[4,128,768]{1,2,0:T(8,128)(2,1)} %stack.32), calls=%async_computation | async-start | bytes 1572864 | tf_op jit(solution)/shard_map/all_to_all | solution.py:197
  520.9 97.9 %reduce-scatter.3.cloned.1.call-start = ((), (), s32[]{:S(2)}) async-start(), calls=%async_computation.13 | async-start | bytes 3932160 | tf_op jit(solution)/shard_map/reduce_scatter | solution.py:34
  574.0 97.3 %reduce-scatter.5.cloned.1.call-start = ((), (), s32[]{:S(2)}) async-start(), calls=%async_computation.14 | async-start | bytes 3932160 | tf_op jit(solution)/shard_map/reduce_scatter | solution.py:34
  595.2 24.8 %copy-start.76 = (f32[128,32]{0,1:T(8,128)S(1)}, f32[128,32]{0,1:T(8,128)}, u32[]{:S(2)}) copy-start(f32[128,32]{0,1:T(8,128)} %copy-done.75) | copy-start | bytes 49156
  595.2 24.8 %copy-start.78 = (f32[128,32]{0,1:T(8,128)S(1)}, f32[128,32]{0,1:T(8,128)}, u32[]{:S(2)}) copy-start(f32[128,32]{0,1:T(8,128)} %copy-done.77) | copy-start | bytes 49156
  595.2 137.1 %all-gather.5.cloned.1.call-start = ((), (), s32[]{:S(2)}) async-start(), calls=%async_computation.15 | async-start | bytes 8355840 | tf_op jit(solution)/shard_map/all_gather | solution.py:40
  630.2 158.5 %all-gather.7.cloned.1.call-start = ((), (), s32[]{:S(2)}) async-start(), calls=%async_computation.16 | async-start | bytes 8355840 | tf_op jit(solution)/shard_map/all_gather | solution.py:40
  689.3 12.5 %all-to-all-start.6 = ((bf16[128,4,192]{0,2,1:T(8,128)(2,1)}), bf16[128,4,192]{0,2,1:T(8,128)(2,1)S(1)}, u32[]{:S(2)}, u32[]{:S(2)}) async-start(bf16[128,4,192]{0,2,1:T(8,128)(2,1)} %copy.141), calls=%async_computation.8 | async-start | bytes 393216 | tf_op jit(solution)/shard_map/all_to_all | solution.py:285
  701.8 34.1 %all-to-all-start.7 = ((bf16[128,4,192]{0,2,1:T(8,128)(2,1)}), bf16[128,4,192]{0,2,1:T(8,128)(2,1)S(1)}, u32[]{:S(2)}, u32[]{:S(2)}) async-start(bf16[128,4,192]{0,2,1:T(8,128)(2,1)} %copy.145), calls=%async_computation.9 | async-start | bytes 393216 | tf_op jit(solution)/shard_map/all_to_all | solution.py:285
  735.9 55.6 %all-to-all-start.2 = ((bf16[128,4,192]{0,2,1:T(8,128)(2,1)}), bf16[128,4,192]{0,2,1:T(8,128)(2,1)S(1)}, u32[]{:S(2)}, u32[]{:S(2)}) async-start(bf16[128,4,192]{0,2,1:T(8,128)(2,1)} %copy.119), calls=%async_computation.4 | async-start | bytes 393216 | tf_op jit(solution)/shard_map/all_to_all | solution.py:278
  791.5 9.6 all-to-all-start.8
  801.1 10.4 all-to-all-start.9
  812.1 10.2 all-to-all-start.4
  822.3 10.9 %all-to-all-start.5 = ((bf16[128,4,192]{0,2,1:T(8,128)(2,1)}), bf16[128,4,192]{0,2,1:T(8,128)(2,1)}, u32[]{:S(2)}, u32[]{:S(2)}) async-start(bf16[128,4,192]{0,2,1:T(8,128)(2,1)} %copy.137), calls=%async_computation.7 | async-start | bytes 393216 | tf_op jit(solution)/shard_map/all_to_all | solution.py:292
  833.2 10.2 all-to-all-start.3
  856.9 208.6 %all-to-all-start.10 = ((f32[64,3,6528]{2,1,0:T(4,128)}), f32[64,3,6528]{2,1,0:T(4,128)}, u32[]{:S(2)}, u32[]{:S(2)}) async-start(f32[64,3,6528]{2,1,0:T(4,128)} %reshape.515), calls=%async_computation.12 | async-start | bytes 13369344 | tf_op jit(solution)/shard_map/all_to_all | solution.py:55
  871.0 190.1 %copy-start.14 = (f32[128,768]{1,0:T(8,128)S(1)}, f32[128,768]{1,0:T(8,128)}, u32[]{:S(2)}) copy-start(f32[128,768]{1,0:T(8,128)} %copy-done.13) | copy-start | bytes 1179652
  871.0 190.1 %copy-start.38 = (bf16[128,1152]{1,0:T(8,128)(2,1)S(1)}, bf16[128,1152]{1,0:T(8,128)(2,1)}, u32[]{:S(2)}) copy-start(bf16[128,1152]{1,0:T(8,128)(2,1)} %get-tuple-element.31) | copy-start | bytes 884740
  (88 other events, 453.8 us)
Sparse Core Ops, SparseCore 0:
  10.5 430.8 all-gather.8
  574.1 44.6 reduce-scatter.2
  621.8 49.4 reduce-scatter.4
  673.0 59.2 all-gather.4
  734.0 54.6 all-gather.6
